TPU v7x, 32 devices: a whole 2x2x4 slice. The times are simulated.
32 devices in a mesh: tm: 4 (over y, core), space: 8 (over z, x).
Axes of the slice: x: 2, y: 2, z: 4, core: 2. Of those that a mesh axis runs over, the one named last changes fastest.
Arguments:
- initial: float32 [24, 192, 256], P('space'), may hold values from -1 to 1
- coarse_guess: float32 [4, 24, 192, 256], P('tm', 'space'), may hold values from -1 to 1
- react_rate: float32 [24, 192, 256], P('space'), may hold values from 0.5 to 3
Outputs:
- corrected: float32 [4, 24, 192, 256], P('tm', 'space')
- defect: float32 [4, 24, 192, 256], P('tm', 'space')
All inputs are finite; a program needn't handle non-finite values.
Results may differ from a plain program's by a relative error of at most 0.00002.
Values sent between devices are 32-bit elements; how exact they have to be, the bound alone decides.
A program may use at most 64 MiB of HBM per device.

v0:
```python
import jax
import jax.numpy as jnp
from jax import lax
from jax.sharding import PartitionSpec as P

STEPS = 3


fine_diffuse = 0.04
fine_growth = 0.05
coarse_diffuse = 0.16
coarse_growth = 0.2


def padded_2(cells, sides, width):
    for axis, dim in sides:
        count = lax.axis_size(axis)
        ends = count - 1
        head = lax.slice_in_dim(cells, 0, width, axis=dim)
        tail = lax.slice_in_dim(cells, cells.shape[dim] - width, cells.shape[dim], axis=dim)
        cells = jnp.concatenate(
            [
                lax.ppermute(tail, axis, [(i, (i + 1) % count) for i in range(ends)]),
                cells,
                lax.ppermute(head, axis, [((i + 1) % count, i) for i in range(ends)]),
            ],
            axis=dim,
        )
    return cells


def from_behind(value, axis, steps):
    count = lax.axis_size(axis)
    leading, last = (max(0, -steps), min(count, count - steps))
    return lax.ppermute(value, axis, [(source, source + steps) for source in range(leading, last)])


def advance(extended, rate_rows, diffuse, growth):
    middle = extended[1:-1]
    padded = jnp.pad(middle, ((0, 0), (1, 1), (1, 1)))
    beside = extended[2:] + extended[:-2]
    beside = beside + padded[:, 2:, 1:-1] + padded[:, :-2, 1:-1]
    beside = beside + padded[:, 1:-1, 2:] + padded[:, 1:-1, :-2]
    return (
        middle
        + diffuse * (beside - 6.0 * middle)
        + growth * rate_rows * (middle - middle * middle * middle)
    )


def coarse_step(current, react_rate):
    extended = padded_2(current, (("space", 0),), 1)
    return advance(extended, react_rate, coarse_diffuse, coarse_growth)


def take_previous(current, initial, tm_index):
    before = from_behind(current, "tm", 1)
    return jnp.where(tm_index == 0, initial, before)


def on_device(initial, coarse_guess, react_rate):
    tm_index = lax.axis_index("tm")
    own_guess = coarse_guess[0]
    first_start = take_previous(own_guess, initial, tm_index)
    planes = react_rate.shape[0]
    length = planes + 2 * STEPS
    rate_wide = padded_2(react_rate, (("space", 0),), STEPS)
    global_rows = lax.axis_index("space") * planes - STEPS + jnp.arange(length)
    inside = ((global_rows >= 0) & (global_rows < planes * lax.axis_size("space"))).astype(
        jnp.float32
    )

    def propagate(start, with_coarse):
        extended = padded_2(start, (("space", 0),), STEPS)
        coarse_part = None
        if with_coarse:
            coarse_part = advance(
                extended[STEPS - 1 : STEPS + planes + 1],
                rate_wide[STEPS : STEPS + planes],
                coarse_diffuse,
                coarse_growth,
            )
        current = extended
        for repeat in range(STEPS):
            rate_rows = rate_wide[repeat + 1 : length - repeat - 1]
            current = advance(current, rate_rows, fine_diffuse, fine_growth)
            current = current * inside[repeat + 1 : length - repeat - 1][:, None, None]
        return (current, coarse_part)

    relaxed, unused = propagate(first_start, False)
    new_start = take_previous(relaxed, initial, tm_index)
    fine_end, coarse_part = propagate(new_start, True)
    defect = fine_end - relaxed
    offset = fine_end - coarse_part

    def chain_turn(interval, current):
        before = take_previous(current, initial, tm_index)
        return coarse_step(before, react_rate) + offset

    corrected = lax.fori_loop(0, lax.axis_size("tm"), chain_turn, jnp.zeros_like(initial))
    return (corrected[None], defect[None])


def solution(mesh):
    in_specs = (P("space", None, None), P("tm", "space", None, None), P("space", None, None))
    out_specs = (P("tm", "space", None, None), P("tm", "space", None, None))
    return jax.shard_map(
        on_device, mesh=mesh, in_specs=in_specs, out_specs=out_specs, check_vma=False
    )
```

profile of v0, /device:TPU:4, one launch (start us, length us, event | category | flops | bytes accessed | tf_op | source)
XLA Modules:
  0.0 203.2 jit_solution(17085572455887937005)
XLA Ops:
  0.6 1.9 collective-permute-start.3
  2.6 4.2 %collective-permute-start.6 = (f32[3,192,256]{2,1,0:T(8,128)}, f32[3,192,256]{2,1,0:T(8,128)}, u32[]{:S(2)}, u32[]{:S(2)}) collective-permute-start(f32[3,192,256]{2,1,0:T(8,128)} %param.7), channel_id=1, source_target_pairs={{0,1},{1,2},{2,3},{3,4},{4,5},{5,6},{6,7},{8,9},{9,10},{10,11},{11... | collective-permute-start | bytes 1769480 | tf_op jit(solution)/shard_map/ppermute | solution.py:23
  8.1 3.9 %collective-permute-done.3 = f32[3,192,256]{2,1,0:T(8,128)S(1)} collective-permute-done((f32[3,192,256]{2,1,0:T(8,128)}, f32[3,192,256]{2,1,0:T(8,128)S(1)}, u32[]{:S(2)}, u32[]{:S(2)}) %collective-permute-start.3) | collective-permute-done | bytes 589856 | tf_op jit(solution)/shard_map/ppermute | solution.py:35
  12.1 3.4 %collective-permute-start.4 = (f32[3,192,256]{2,1,0:T(8,128)S(1)}, f32[3,192,256]{2,1,0:T(8,128)S(1)}, u32[]{:S(2)}, u32[]{:S(2)}) collective-permute-start(f32[3,192,256]{2,1,0:T(8,128)S(1)} %broadcast_select_fusion.3), channel_id=1, source_target_pairs={{0,1},{1,2},{2,3},{3,4},{4,5},{5,6},{6,7},{8,9},{9,10},{10,11},{11... | collective-permute-start | bytes 1769480 | tf_op jit(solution)/shard_map/ppermute | solution.py:23
  17.1 28.2 %collective-permute-done.6 = f32[3,192,256]{2,1,0:T(8,128)} collective-permute-done((f32[3,192,256]{2,1,0:T(8,128)}, f32[3,192,256]{2,1,0:T(8,128)}, u32[]{:S(2)}, u32[]{:S(2)}) %collective-permute-start.6) | collective-permute-done | bytes 589856 | tf_op jit(solution)/shard_map/ppermute | solution.py:23
  47.5 8.5 %collective-permute-done.4 = f32[3,192,256]{2,1,0:T(8,128)S(1)} collective-permute-done((f32[3,192,256]{2,1,0:T(8,128)S(1)}, f32[3,192,256]{2,1,0:T(8,128)S(1)}, u32[]{:S(2)}, u32[]{:S(2)}) %collective-permute-start.4) | collective-permute-done | bytes 589856 | tf_op jit(solution)/shard_map/ppermute | solution.py:23
  59.9 1.9 collective-permute-start.8
  61.8 9.4 %collective-permute-done.8 = f32[3,192,256]{2,1,0:T(8,128)S(1)} collective-permute-done((f32[3,192,256]{2,1,0:T(8,128)S(1)}, f32[3,192,256]{2,1,0:T(8,128)S(1)}, u32[]{:S(2)}, u32[]{:S(2)}) %collective-permute-start.8) | collective-permute-done | bytes 589856 | tf_op jit(solution)/shard_map/ppermute | solution.py:35
  72.6 5.7 %collective-permute-start.9 = (f32[3,192,256]{2,1,0:T(8,128)S(1)}, f32[3,192,256]{2,1,0:T(8,128)}, u32[]{:S(2)}, u32[]{:S(2)}) collective-permute-start(f32[3,192,256]{2,1,0:T(8,128)S(1)} %broadcast_select_fusion.2), channel_id=1, source_target_pairs={{0,1},{1,2},{2,3},{3,4},{4,5},{5,6},{6,7},{8,9},{9,10},{10,11},{11... | collective-permute-start | bytes 1769480 | tf_op jit(solution)/shard_map/ppermute | solution.py:23
  78.3 5.2 %collective-permute-done.10 = f32[3,192,256]{2,1,0:T(8,128)} collective-permute-done((f32[3,192,256]{2,1,0:T(8,128)S(1)}, f32[3,192,256]{2,1,0:T(8,128)}, u32[]{:S(2)}, u32[]{:S(2)}) %collective-permute-start.10) | collective-permute-done | bytes 589856 | tf_op jit(solution)/shard_map/ppermute | solution.py:25
  83.6 11.0 %collective-permute-done.9 = f32[3,192,256]{2,1,0:T(8,128)} collective-permute-done((f32[3,192,256]{2,1,0:T(8,128)S(1)}, f32[3,192,256]{2,1,0:T(8,128)}, u32[]{:S(2)}, u32[]{:S(2)}) %collective-permute-start.9) | collective-permute-done | bytes 589856 | tf_op jit(solution)/shard_map/ppermute | solution.py:23
  102.0 101.3 %while.13 = (s32[]{:T(128)}, f32[3,192,256]{2,1,0:T(8,128)}, pred[]{:T(512)}, f32[3,192,256]{2,1,0:T(8,128)S(1)}, f32[3,192,256]{2,1,0:T(8,128)S(1)}, /*index=5*/f32[3,192,256]{2,1,0:T(8,128)S(1)}, s32[]{:T(128)}, s32[]{:T(128)}) while((s32[]{:T(128)}, f32[3,192,256]{2,1,0:T(8,128)}, pred[]{:T(512)}, f32[3,192,256]{2,1,0:T(8,128)S(1)}, ...), condition=%wide.region_1.2_spmd.clone, body=%wide.region_0.1_spmd.clone.sunk | while | flops 2949123 | bytes 10420440 | solution.py:100
  102.0 1.9 collective-permute-start
  104.0 9.9 %collective-permute-done = f32[3,192,256]{2,1,0:T(8,128)S(1)} collective-permute-done((f32[3,192,256]{2,1,0:T(8,128)S(1)}, f32[3,192,256]{2,1,0:T(8,128)S(1)}, u32[]{:S(2)}, u32[]{:S(2)}) %collective-permute-start) | collective-permute-done | bytes 589856 | tf_op jit(solution)/shard_map/while/body/eval_jaxpr/ppermute | solution.py:35
  114.0 4.3 %collective-permute-start.1 = (f32[1,192,256]{2,1,0:T(8,128)S(1)}, f32[1,192,256]{2,1,0:T(8,128)S(1)}, u32[]{:S(2)}, u32[]{:S(2)}) collective-permute-start(f32[1,192,256]{2,1,0:T(8,128)S(1)} %get-tuple-element.158), channel_id=1, source_target_pairs={{0,1},{1,2},{2,3},{3,4},{4,5},{5,6},{6,7},{8,9},{9,10},{10,11},{11... | collective-permute-start | bytes 589832 | tf_op jit(solution)/shard_map/while/body/eval_jaxpr/ppermute | solution.py:23
  119.6 1.9 collective-permute-done.1
  121.4 4.4 %collective-permute-done.2 = f32[1,192,256]{2,1,0:T(8,128)S(1)} collective-permute-done((f32[1,192,256]{2,1,0:T(8,128)S(1)}, f32[1,192,256]{2,1,0:T(8,128)S(1)}, u32[]{:S(2)}, u32[]{:S(2)}) %collective-permute-start.2) | collective-permute-done | bytes 196640 | tf_op jit(solution)/shard_map/while/body/eval_jaxpr/ppermute | solution.py:25
  128.2 1.9 collective-permute-start
  130.2 9.3 %collective-permute-done = f32[3,192,256]{2,1,0:T(8,128)S(1)} collective-permute-done((f32[3,192,256]{2,1,0:T(8,128)S(1)}, f32[3,192,256]{2,1,0:T(8,128)S(1)}, u32[]{:S(2)}, u32[]{:S(2)}) %collective-permute-start) | collective-permute-done | bytes 589856 | tf_op jit(solution)/shard_map/while/body/eval_jaxpr/ppermute | solution.py:35
  139.6 4.5 %collective-permute-start.1 = (f32[1,192,256]{2,1,0:T(8,128)S(1)}, f32[1,192,256]{2,1,0:T(8,128)S(1)}, u32[]{:S(2)}, u32[]{:S(2)}) collective-permute-start(f32[1,192,256]{2,1,0:T(8,128)S(1)} %get-tuple-element.158), channel_id=1, source_target_pairs={{0,1},{1,2},{2,3},{3,4},{4,5},{5,6},{6,7},{8,9},{9,10},{10,11},{11... | collective-permute-start | bytes 589832 | tf_op jit(solution)/shard_map/while/body/eval_jaxpr/ppermute | solution.py:23
  145.4 1.9 collective-permute-done.1
  147.2 4.4 %collective-permute-done.2 = f32[1,192,256]{2,1,0:T(8,128)S(1)} collective-permute-done((f32[1,192,256]{2,1,0:T(8,128)S(1)}, f32[1,192,256]{2,1,0:T(8,128)S(1)}, u32[]{:S(2)}, u32[]{:S(2)}) %collective-permute-start.2) | collective-permute-done | bytes 196640 | tf_op jit(solution)/shard_map/while/body/eval_jaxpr/ppermute | solution.py:25
  154.0 1.9 collective-permute-start
  156.0 9.3 %collective-permute-done = f32[3,192,256]{2,1,0:T(8,128)S(1)} collective-permute-done((f32[3,192,256]{2,1,0:T(8,128)S(1)}, f32[3,192,256]{2,1,0:T(8,128)S(1)}, u32[]{:S(2)}, u32[]{:S(2)}) %collective-permute-start) | collective-permute-done | bytes 589856 | tf_op jit(solution)/shard_map/while/body/eval_jaxpr/ppermute | solution.py:35
  165.3 3.2 %collective-permute-start.1 = (f32[1,192,256]{2,1,0:T(8,128)S(1)}, f32[1,192,256]{2,1,0:T(8,128)S(1)}, u32[]{:S(2)}, u32[]{:S(2)}) collective-permute-start(f32[1,192,256]{2,1,0:T(8,128)S(1)} %get-tuple-element.158), channel_id=1, source_target_pairs={{0,1},{1,2},{2,3},{3,4},{4,5},{5,6},{6,7},{8,9},{9,10},{10,11},{11... | collective-permute-start | bytes 589832 | tf_op jit(solution)/shard_map/while/body/eval_jaxpr/ppermute | solution.py:23
  169.9 1.9 collective-permute-done.1
  171.8 4.4 %collective-permute-done.2 = f32[1,192,256]{2,1,0:T(8,128)S(1)} collective-permute-done((f32[1,192,256]{2,1,0:T(8,128)S(1)}, f32[1,192,256]{2,1,0:T(8,128)S(1)}, u32[]{:S(2)}, u32[]{:S(2)}) %collective-permute-start.2) | collective-permute-done | bytes 196640 | tf_op jit(solution)/shard_map/while/body/eval_jaxpr/ppermute | solution.py:25
  178.6 1.9 collective-permute-start
  180.5 9.3 %collective-permute-done = f32[3,192,256]{2,1,0:T(8,128)S(1)} collective-permute-done((f32[3,192,256]{2,1,0:T(8,128)S(1)}, f32[3,192,256]{2,1,0:T(8,128)S(1)}, u32[]{:S(2)}, u32[]{:S(2)}) %collective-permute-start) | collective-permute-done | bytes 589856 | tf_op jit(solution)/shard_map/while/body/eval_jaxpr/ppermute | solution.py:35
  189.9 4.5 %collective-permute-start.1 = (f32[1,192,256]{2,1,0:T(8,128)S(1)}, f32[1,192,256]{2,1,0:T(8,128)S(1)}, u32[]{:S(2)}, u32[]{:S(2)}) collective-permute-start(f32[1,192,256]{2,1,0:T(8,128)S(1)} %get-tuple-element.158), channel_id=1, source_target_pairs={{0,1},{1,2},{2,3},{3,4},{4,5},{5,6},{6,7},{8,9},{9,10},{10,11},{11... | collective-permute-start | bytes 589832 | tf_op jit(solution)/shard_map/while/body/eval_jaxpr/ppermute | solution.py:23
  195.7 1.9 collective-permute-done.1
  197.5 4.4 %collective-permute-done.2 = f32[1,192,256]{2,1,0:T(8,128)S(1)} collective-permute-done((f32[1,192,256]{2,1,0:T(8,128)S(1)}, f32[1,192,256]{2,1,0:T(8,128)S(1)}, u32[]{:S(2)}, u32[]{:S(2)}) %collective-permute-start.2) | collective-permute-done | bytes 196640 | tf_op jit(solution)/shard_map/while/body/eval_jaxpr/ppermute | solution.py:25
  (58 shorter events, 31.7 us)
Async XLA Ops:
  0.6 11.4 %collective-permute-start.3 = (f32[3,192,256]{2,1,0:T(8,128)}, f32[3,192,256]{2,1,0:T(8,128)S(1)}, u32[]{:S(2)}, u32[]{:S(2)}) collective-permute-start(f32[3,192,256]{2,1,0:T(8,128)} %bitcast.4), channel_id=1, source_target_pairs={{0,8},{8,16},{16,24},{1,9},{9,17},{17,25},{2,10},{10,18},{18,26},{... | collective-permute-start | bytes 1769480 | tf_op jit(solution)/shard_map/ppermute | solution.py:35
  2.6 42.7 %collective-permute-start.6 = (f32[3,192,256]{2,1,0:T(8,128)}, f32[3,192,256]{2,1,0:T(8,128)}, u32[]{:S(2)}, u32[]{:S(2)}) collective-permute-start(f32[3,192,256]{2,1,0:T(8,128)} %param.7), channel_id=1, source_target_pairs={{0,1},{1,2},{2,3},{3,4},{4,5},{5,6},{6,7},{8,9},{9,10},{10,11},{11... | collective-permute-start | bytes 1769480 | tf_op jit(solution)/shard_map/ppermute | solution.py:23
  6.8 39.6 %collective-permute-start.7 = (f32[3,192,256]{2,1,0:T(8,128)}, f32[3,192,256]{2,1,0:T(8,128)}, u32[]{:S(2)}, u32[]{:S(2)}) collective-permute-start(f32[3,192,256]{2,1,0:T(8,128)} %param.7), channel_id=1, source_target_pairs={{1,0},{2,1},{3,2},{4,3},{5,4},{6,5},{7,6},{9,8},{10,9},{11,10},{12... | collective-permute-start | bytes 1769480 | tf_op jit(solution)/shard_map/ppermute | solution.py:25
  8.1 38.3 %copy-start = (f32[3,192,256]{2,1,0:T(8,128)S(1)}, f32[3,192,256]{2,1,0:T(8,128)}, u32[]{:S(2)}) copy-start(f32[3,192,256]{2,1,0:T(8,128)} %param.7) | copy-start | bytes 1769476
  12.1 43.9 %collective-permute-start.4 = (f32[3,192,256]{2,1,0:T(8,128)S(1)}, f32[3,192,256]{2,1,0:T(8,128)S(1)}, u32[]{:S(2)}, u32[]{:S(2)}) collective-permute-start(f32[3,192,256]{2,1,0:T(8,128)S(1)} %broadcast_select_fusion.3), channel_id=1, source_target_pairs={{0,1},{1,2},{2,3},{3,4},{4,5},{5,6},{6,7},{8,9},{9,10},{10,11},{11... | collective-permute-start | bytes 1769480 | tf_op jit(solution)/shard_map/ppermute | solution.py:23
  15.6 40.5 %collective-permute-start.5 = (f32[3,192,256]{2,1,0:T(8,128)S(1)}, f32[3,192,256]{2,1,0:T(8,128)}, u32[]{:S(2)}, u32[]{:S(2)}) collective-permute-start(f32[3,192,256]{2,1,0:T(8,128)S(1)} %broadcast_select_fusion.3), channel_id=1, source_target_pairs={{1,0},{2,1},{3,2},{4,3},{5,4},{6,5},{7,6},{9,8},{10,9},{11,10},{12... | collective-permute-start | bytes 1769480 | tf_op jit(solution)/shard_map/ppermute | solution.py:25
  59.4 11.9 %copy-start.1 = (f32[3,192,256]{2,1,0:T(8,128)S(1)}, f32[3,192,256]{2,1,0:T(8,128)}, u32[]{:S(2)}) copy-start(f32[3,192,256]{2,1,0:T(8,128)} %param.5) | copy-start | bytes 1769476
  59.9 11.4 %copy-start.2 = (f32[3,192,256]{2,1,0:T(8,128)}, f32[3,192,256]{2,1,0:T(8,128)S(1)}, u32[]{:S(2)}) copy-start(f32[3,192,256]{2,1,0:T(8,128)S(1)} %fusion.53) | copy-start | bytes 1769476
  59.9 11.3 %collective-permute-start.8 = (f32[3,192,256]{2,1,0:T(8,128)S(1)}, f32[3,192,256]{2,1,0:T(8,128)S(1)}, u32[]{:S(2)}, u32[]{:S(2)}) collective-permute-start(f32[3,192,256]{2,1,0:T(8,128)S(1)} %fusion.53), channel_id=1, source_target_pairs={{0,8},{8,16},{16,24},{1,9},{9,17},{17,25},{2,10},{10,18},{18,26},{... | collective-permute-start | bytes 1769480 | tf_op jit(solution)/shard_map/ppermute | solution.py:35
  71.3 12.2 %collective-permute-start.10 = (f32[3,192,256]{2,1,0:T(8,128)S(1)}, f32[3,192,256]{2,1,0:T(8,128)}, u32[]{:S(2)}, u32[]{:S(2)}) collective-permute-start(f32[3,192,256]{2,1,0:T(8,128)S(1)} %broadcast_select_fusion.2), channel_id=1, source_target_pairs={{1,0},{2,1},{3,2},{4,3},{5,4},{6,5},{7,6},{9,8},{10,9},{11,10},{12... | collective-permute-start | bytes 1769480 | tf_op jit(solution)/shard_map/ppermute | solution.py:25
  72.6 22.0 %collective-permute-start.9 = (f32[3,192,256]{2,1,0:T(8,128)S(1)}, f32[3,192,256]{2,1,0:T(8,128)}, u32[]{:S(2)}, u32[]{:S(2)}) collective-permute-start(f32[3,192,256]{2,1,0:T(8,128)S(1)} %broadcast_select_fusion.2), channel_id=1, source_target_pairs={{0,1},{1,2},{2,3},{3,4},{4,5},{5,6},{6,7},{8,9},{9,10},{10,11},{11... | collective-permute-start | bytes 1769480 | tf_op jit(solution)/shard_map/ppermute | solution.py:23
  98.0 1.1 copy-start.3
  102.0 11.8 %collective-permute-start = (f32[3,192,256]{2,1,0:T(8,128)S(1)}, f32[3,192,256]{2,1,0:T(8,128)S(1)}, u32[]{:S(2)}, u32[]{:S(2)}) collective-permute-start(f32[3,192,256]{2,1,0:T(8,128)S(1)} %broadcast_select_fusion.6), channel_id=1, source_target_pairs={{0,8},{8,16},{16,24},{1,9},{9,17},{17,25},{2,10},{10,18},{18,26},{... | collective-permute-start | bytes 1769480 | tf_op jit(solution)/shard_map/while/body/eval_jaxpr/ppermute | solution.py:35
  114.0 7.5 %collective-permute-start.1 = (f32[1,192,256]{2,1,0:T(8,128)S(1)}, f32[1,192,256]{2,1,0:T(8,128)S(1)}, u32[]{:S(2)}, u32[]{:S(2)}) collective-permute-start(f32[1,192,256]{2,1,0:T(8,128)S(1)} %get-tuple-element.158), channel_id=1, source_target_pairs={{0,1},{1,2},{2,3},{3,4},{4,5},{5,6},{6,7},{8,9},{9,10},{10,11},{11... | collective-permute-start | bytes 589832 | tf_op jit(solution)/shard_map/while/body/eval_jaxpr/ppermute | solution.py:23
  118.3 7.6 %collective-permute-start.2 = (f32[1,192,256]{2,1,0:T(8,128)S(1)}, f32[1,192,256]{2,1,0:T(8,128)S(1)}, u32[]{:S(2)}, u32[]{:S(2)}) collective-permute-start(f32[1,192,256]{2,1,0:T(8,128)S(1)} %get-tuple-element.159), channel_id=1, source_target_pairs={{1,0},{2,1},{3,2},{4,3},{5,4},{6,5},{7,6},{9,8},{10,9},{11,10},{12... | collective-permute-start | bytes 589832 | tf_op jit(solution)/shard_map/while/body/eval_jaxpr/ppermute | solution.py:25
  128.2 11.2 %collective-permute-start = (f32[3,192,256]{2,1,0:T(8,128)S(1)}, f32[3,192,256]{2,1,0:T(8,128)S(1)}, u32[]{:S(2)}, u32[]{:S(2)}) collective-permute-start(f32[3,192,256]{2,1,0:T(8,128)S(1)} %broadcast_select_fusion.6), channel_id=1, source_target_pairs={{0,8},{8,16},{16,24},{1,9},{9,17},{17,25},{2,10},{10,18},{18,26},{... | collective-permute-start | bytes 1769480 | tf_op jit(solution)/shard_map/while/body/eval_jaxpr/ppermute | solution.py:35
  139.6 7.7 %collective-permute-start.1 = (f32[1,192,256]{2,1,0:T(8,128)S(1)}, f32[1,192,256]{2,1,0:T(8,128)S(1)}, u32[]{:S(2)}, u32[]{:S(2)}) collective-permute-start(f32[1,192,256]{2,1,0:T(8,128)S(1)} %get-tuple-element.158), channel_id=1, source_target_pairs={{0,1},{1,2},{2,3},{3,4},{4,5},{5,6},{6,7},{8,9},{9,10},{10,11},{11... | collective-permute-start | bytes 589832 | tf_op jit(solution)/shard_map/while/body/eval_jaxpr/ppermute | solution.py:23
  144.1 7.6 %collective-permute-start.2 = (f32[1,192,256]{2,1,0:T(8,128)S(1)}, f32[1,192,256]{2,1,0:T(8,128)S(1)}, u32[]{:S(2)}, u32[]{:S(2)}) collective-permute-start(f32[1,192,256]{2,1,0:T(8,128)S(1)} %get-tuple-element.159), channel_id=1, source_target_pairs={{1,0},{2,1},{3,2},{4,3},{5,4},{6,5},{7,6},{9,8},{10,9},{11,10},{12... | collective-permute-start | bytes 589832 | tf_op jit(solution)/shard_map/while/body/eval_jaxpr/ppermute | solution.py:25
  154.0 11.2 %collective-permute-start = (f32[3,192,256]{2,1,0:T(8,128)S(1)}, f32[3,192,256]{2,1,0:T(8,128)S(1)}, u32[]{:S(2)}, u32[]{:S(2)}) collective-permute-start(f32[3,192,256]{2,1,0:T(8,128)S(1)} %broadcast_select_fusion.6), channel_id=1, source_target_pairs={{0,8},{8,16},{16,24},{1,9},{9,17},{17,25},{2,10},{10,18},{18,26},{... | collective-permute-start | bytes 1769480 | tf_op jit(solution)/shard_map/while/body/eval_jaxpr/ppermute | solution.py:35
  165.3 6.4 %collective-permute-start.1 = (f32[1,192,256]{2,1,0:T(8,128)S(1)}, f32[1,192,256]{2,1,0:T(8,128)S(1)}, u32[]{:S(2)}, u32[]{:S(2)}) collective-permute-start(f32[1,192,256]{2,1,0:T(8,128)S(1)} %get-tuple-element.158), channel_id=1, source_target_pairs={{0,1},{1,2},{2,3},{3,4},{4,5},{5,6},{6,7},{8,9},{9,10},{10,11},{11... | collective-permute-start | bytes 589832 | tf_op jit(solution)/shard_map/while/body/eval_jaxpr/ppermute | solution.py:23
  168.6 7.6 %collective-permute-start.2 = (f32[1,192,256]{2,1,0:T(8,128)S(1)}, f32[1,192,256]{2,1,0:T(8,128)S(1)}, u32[]{:S(2)}, u32[]{:S(2)}) collective-permute-start(f32[1,192,256]{2,1,0:T(8,128)S(1)} %get-tuple-element.159), channel_id=1, source_target_pairs={{1,0},{2,1},{3,2},{4,3},{5,4},{6,5},{7,6},{9,8},{10,9},{11,10},{12... | collective-permute-start | bytes 589832 | tf_op jit(solution)/shard_map/while/body/eval_jaxpr/ppermute | solution.py:25
  178.6 11.2 %collective-permute-start = (f32[3,192,256]{2,1,0:T(8,128)S(1)}, f32[3,192,256]{2,1,0:T(8,128)S(1)}, u32[]{:S(2)}, u32[]{:S(2)}) collective-permute-start(f32[3,192,256]{2,1,0:T(8,128)S(1)} %broadcast_select_fusion.6), channel_id=1, source_target_pairs={{0,8},{8,16},{16,24},{1,9},{9,17},{17,25},{2,10},{10,18},{18,26},{... | collective-permute-start | bytes 1769480 | tf_op jit(solution)/shard_map/while/body/eval_jaxpr/ppermute | solution.py:35
  189.9 7.7 %collective-permute-start.1 = (f32[1,192,256]{2,1,0:T(8,128)S(1)}, f32[1,192,256]{2,1,0:T(8,128)S(1)}, u32[]{:S(2)}, u32[]{:S(2)}) collective-permute-start(f32[1,192,256]{2,1,0:T(8,128)S(1)} %get-tuple-element.158), channel_id=1, source_target_pairs={{0,1},{1,2},{2,3},{3,4},{4,5},{5,6},{6,7},{8,9},{9,10},{10,11},{11... | collective-permute-start | bytes 589832 | tf_op jit(solution)/shard_map/while/body/eval_jaxpr/ppermute | solution.py:23
  194.4 7.6 %collective-permute-start.2 = (f32[1,192,256]{2,1,0:T(8,128)S(1)}, f32[1,192,256]{2,1,0:T(8,128)S(1)}, u32[]{:S(2)}, u32[]{:S(2)}) collective-permute-start(f32[1,192,256]{2,1,0:T(8,128)S(1)} %get-tuple-element.159), channel_id=1, source_target_pairs={{1,0},{2,1},{3,2},{4,3},{5,4},{6,5},{7,6},{9,8},{10,9},{11,10},{12... | collective-permute-start | bytes 589832 | tf_op jit(solution)/shard_map/while/body/eval_jaxpr/ppermute | solution.py:25
where the time goes:
time: 204 us; the launch traced here: 203 us
  waiting for transfers between devices  129 us (63%)
  starting transfers between devices  50.5 us (25%)
  other arithmetic  18.6 us (9%)
  local copies, waits for them, and re-layouts  4.06 us (2%)
    ppermute x7, waiting for transfers between devices, padded_2(): lax.ppermute(tail, axis, [(i, (i + 1) % count) for i in range(ends)])  55.1 us
    ppermute x6, waiting for transfers between devices, from_behind(): lax.ppermute(value, axis, [(source, source + steps) for source in range(l...  51 us
    ppermute x7, starting transfers between devices, padded_2(): lax.ppermute(tail, axis, [(i, (i + 1) % count) for i in range(ends)])  30 us
    ppermute x7, waiting for transfers between devices, padded_2(): lax.ppermute(head, axis, [((i + 1) % count, i) for i in range(ends)])  22.8 us
    ppermute x6, starting transfers between devices, from_behind(): lax.ppermute(value, axis, [(source, source + steps) for source in range(l...  11.5 us
    ppermute x7, starting transfers between devices, padded_2(): lax.ppermute(head, axis, [((i + 1) % count, i) for i in range(ends)])  9.03 us
    add x4, other arithmetic, chain_turn(): return coarse_step(before, react_rate) + offset  5.13 us
    mul x5, other arithmetic, propagate(): current = current * inside[repeat + 1:length - repeat - 1][:, None, None]  4.2 us
  transfers between devices with their start and end apart: 20, of which 18 were waited for; matrix products, arithmetic and copies ran while one was open for 1% of the time, Pallas kernels for 0%

commit v1 on v0

v1 whole, which is shorter than its diff:
```python
import functools

import jax
import jax.numpy as jnp
from jax import lax
from jax.experimental import pallas as pl
from jax.experimental.pallas import tpu as pltpu
from jax.sharding import PartitionSpec as P

STEPS = 3
SUBLANES = 8

fine_diffuse = 0.04
fine_growth = 0.05
coarse_ratio = 4.0

MESH = pl.DeviceIdType.MESH

START, RATE, AGAIN, CHAIN, DEFECT, CORRECTED = 0, 4, 8, 11, 14, 15
COPIES = 16


def kernel(
    nt, ns, planes, half, wide,
    initial, guess, rate_in, corrected_out, defect_out,
    start, rate, again, before, first, second, relaxed, coarse, offset, defect, after, reach,
    send, recv, local,
):
    tm, space = lax.axis_index("tm"), lax.axis_index("space")
    pair, side = lax.div(space, 2), lax.rem(space, 2)
    pairs = ns // 2
    mate = space + 1 - 2 * side
    block = 2 * planes
    length = block + 2 * STEPS
    rows = half + 2 * wide
    has_low, has_high = pair > 0, pair < pairs - 1
    has_next, has_previous = tm < nt - 1, tm > 0
    own = pl.ds(STEPS, block)

    for ref in (start, rate, again, before):
        zero_plane = jnp.zeros((STEPS,) + ref.shape[1:], jnp.float32)
        zero_rows = jnp.zeros((block, wide, ref.shape[2]), jnp.float32)
        ref[0:STEPS] = zero_plane
        ref[STEPS + block : length] = zero_plane
        ref[STEPS : STEPS + block, 0:wide] = zero_rows
        ref[STEPS : STEPS + block, wide + half : rows] = zero_rows

    barrier = pltpu.get_barrier_semaphore()
    count = jnp.int32(0)
    for step in (-1, 0, 1):
        for place in ("own", "mate", "low", "high"):
            if step == 0 and place == "own":
                continue
            there = {"own": space, "mate": mate, "low": space - 2, "high": space + 2}[place]
            tests = []
            if step:
                tests.append(has_next if step > 0 else has_previous)
            if place in ("low", "high"):
                tests.append(has_low if place == "low" else has_high)
            target = {"tm": tm + step, "space": there}
            if tests:
                valid = functools.reduce(jnp.logical_and, tests)

                @pl.when(valid)
                def _(target=target):
                    pl.semaphore_signal(barrier, inc=1, device_id=target, device_id_type=MESH)

                count = count + valid.astype(jnp.int32)
            else:
                pl.semaphore_signal(barrier, inc=1, device_id=target, device_id_type=MESH)
                count = count + 1
    pl.semaphore_wait(barrier, count)

    def remote(src, dst, slot, to_tm, to_space):
        return pltpu.make_async_remote_copy(
            src_ref=src,
            dst_ref=dst,
            send_sem=send.at[slot],
            recv_sem=recv.at[slot],
            device_id={"tm": to_tm, "space": to_space},
            device_id_type=MESH,
        )

    def cut(ref, target):
        return ref.at[:, pl.ds(pl.multiple_of(target * (half - wide), SUBLANES), half + wide), :]

    def spot(ref, target, begin, size):
        at = pl.multiple_of(wide * (1 - target), SUBLANES)
        return ref.at[pl.ds(begin, size), pl.ds(at, half + wide), :]

    slab = STEPS + planes * side
    other = STEPS + planes * (1 - side)

    rate_own = pltpu.make_async_copy(cut(rate_in, side), spot(rate, side, slab, planes), local.at[0])
    rate_mate = remote(
        cut(rate_in, 1 - side), spot(rate, 1 - side, slab, planes), RATE, tm, mate
    )
    initial_own = pltpu.make_async_copy(cut(initial, side), spot(start, side, slab, planes), local.at[1])
    initial_mate = remote(
        cut(initial, 1 - side), spot(start, 1 - side, slab, planes), START, tm, mate
    )
    guess_mate = remote(
        cut(guess, 1 - side), spot(start, 1 - side, slab, planes), START + 3, tm + 1, mate
    )
    guess_own = remote(
        cut(guess, side), spot(start, side, slab, planes), START + 2, tm + 1, space
    )

    @pl.when(tm == 0)
    def _():
        initial_mate.start()
        initial_own.start()

    @pl.when(has_next)
    def _():
        guess_mate.start()
        guess_own.start()

    rate_own.start()
    rate_mate.start()

    for ref in (first, second):
        @pl.when(jnp.logical_not(has_low))
        def _(ref=ref):
            ref[0:STEPS] = jnp.zeros((STEPS,) + ref.shape[1:], jnp.float32)

        @pl.when(jnp.logical_not(has_high))
        def _(ref=ref):
            ref[STEPS + block : length] = jnp.zeros((STEPS,) + ref.shape[1:], jnp.float32)

    row = lax.broadcasted_iota(jnp.int32, reach.shape, 0)
    outside = jnp.logical_or(
        jnp.logical_and(side == 0, row < wide), jnp.logical_and(side == 1, row >= wide + half)
    )
    reach[...] = jnp.where(outside, 0.0, fine_diffuse)

    def edges(ref, width, slot, to_tm):
        low = remote(
            spot(ref, side, STEPS, width), spot(ref, side, STEPS + block, width), slot, to_tm, space - 2
        )
        high = remote(
            spot(ref, side, STEPS + block - width, width),
            spot(ref, side, STEPS - width, width),
            slot + 1,
            to_tm,
            space + 2,
        )
        return low, high

    def send_edge(low, high, which):
        @pl.when(jnp.logical_and(which == 0, has_low))
        def _():
            low.start()

        @pl.when(jnp.logical_and(which == 1, has_high))
        def _():
            high.start()

    start_low, start_high = edges(start, STEPS, COPIES, tm)
    rate_low, rate_high = edges(rate, STEPS - 1, RATE + 1, tm)

    rate_own.wait()
    send_edge(rate_low, rate_high, side)

    @pl.when(tm == 0)
    def _():
        initial_own.wait()

    @pl.when(has_previous)
    def _():
        guess_own.wait_recv()

    send_edge(start_low, start_high, side)

    @pl.when(tm == 0)
    def _():
        initial_mate.wait_recv()

    @pl.when(has_previous)
    def _():
        guess_mate.wait_recv()

    send_edge(start_low, start_high, 1 - side)
    rate_mate.wait_recv()
    send_edge(rate_low, rate_high, 1 - side)

    @pl.when(has_high)
    def _():
        rate_low.wait_recv()
        start_low.wait_recv()

    @pl.when(has_low)
    def _():
        rate_high.wait_recv()
        start_high.wait_recv()

    keep = pltpu.make_async_copy(start, again, local.at[1])

    @pl.when(tm == 0)
    def _():
        keep.start()

    width = start.shape[2]
    lane = lax.broadcasted_iota(jnp.int32, reach.shape, 1)

    def change(ref, z):
        middle = ref[z]
        beside = ref[z + 1] + ref[z - 1]
        beside = beside + pltpu.roll(middle, 1, 0) + pltpu.roll(middle, rows - 1, 0)
        beside = beside + jnp.where(lane == 0, 0.0, pltpu.roll(middle, 1, 1))
        beside = beside + jnp.where(lane == width - 1, 0.0, pltpu.roll(middle, width - 1, 1))
        growth = rate[z] * (fine_growth - fine_growth * (middle * middle))
        return middle, reach[...] * beside + middle * (growth - 6.0 * fine_diffuse)

    def span(step):
        low = jnp.where(has_low, step, max(step, STEPS))
        high = jnp.where(has_high, length - step, min(length - step, STEPS + block))
        return low, high

    def fine(src, dst, step):
        def plane(z, carry):
            middle, delta = change(src, z)
            dst[z] = middle + delta
            return carry

        lax.fori_loop(*span(step), plane, 0)

    fine(start, first, 1)
    fine(first, second, 2)
    fine(second, relaxed, 3)

    def give(src, dst, width, slot):
        whole = remote(
            spot(src, side, STEPS, block), spot(dst, side, STEPS, block), slot, tm + 1, space
        )
        low = remote(
            spot(src, side, STEPS, width), spot(dst, side, STEPS + block, width), slot + 1, tm + 1, space - 2
        )
        high = remote(
            spot(src, side, STEPS + block - width, width),
            spot(dst, side, STEPS - width, width),
            slot + 2,
            tm + 1,
            space + 2,
        )
        return whole, low, high

    def begin(copies, valid):
        whole, low, high = copies
        pl.when(jnp.logical_and(valid, has_low))(low.start)
        pl.when(jnp.logical_and(valid, has_high))(high.start)
        pl.when(valid)(whole.start)

    def sent(copies, valid):
        whole, low, high = copies
        pl.when(jnp.logical_and(valid, has_low))(low.wait_send)
        pl.when(jnp.logical_and(valid, has_high))(high.wait_send)
        pl.when(valid)(whole.wait_send)

    def received(copies, valid):
        whole, low, high = copies
        pl.when(jnp.logical_and(valid, has_high))(low.wait_recv)
        pl.when(jnp.logical_and(valid, has_low))(high.wait_recv)
        pl.when(valid)(whole.wait_recv)

    given = give(relaxed, again, STEPS, AGAIN)
    begin(given, has_next)

    @pl.when(tm == 0)
    def _():
        keep.wait()

    received(given, has_previous)

    def first_plane(z, carry):
        middle, delta = change(again, z)
        first[z] = middle + delta
        coarse[z] = middle + coarse_ratio * delta
        return carry

    lax.fori_loop(*span(1), first_plane, 0)
    fine(first, second, 2)

    def last_plane(z, carry):
        middle, delta = change(second, z)
        end = middle + delta
        defect[z] = end - relaxed[z]
        shift = end - coarse[z]
        offset[z] = shift
        after[z] = coarse[z] + shift
        return carry

    lax.fori_loop(STEPS, STEPS + block, last_plane, 0)

    def back(src, dst, slot, lane_slot):
        mine = pl.ds(pl.multiple_of(side * half, SUBLANES), half)
        middle_rows = pl.ds(wide, half)
        stay = pltpu.make_async_copy(
            src.at[pl.ds(slab, planes), middle_rows, :], dst.at[:, mine, :], local.at[lane_slot]
        )
        go = remote(
            src.at[pl.ds(other, planes), middle_rows, :], dst.at[:, mine, :], slot, tm, mate
        )
        return stay, go

    defect_stay, defect_go = back(defect, defect_out, DEFECT, 2)

    passed = give(after, before, 1, CHAIN)
    later = tm > 1
    received(passed, later)

    @pl.when(later)
    def _():
        def plane(z, carry):
            middle, delta = change(before, z)
            after[z] = middle + coarse_ratio * delta + offset[z]
            return carry

        lax.fori_loop(STEPS, STEPS + block, plane, 0)

    onward = jnp.logical_and(tm > 0, has_next)
    begin(passed, onward)
    defect_go.start()
    defect_stay.start()
    corrected_stay, corrected_go = back(after, corrected_out, CORRECTED, 3)
    corrected_go.start()
    corrected_stay.start()

    @pl.when(tm == 0)
    def _():
        initial_mate.wait_send()

    @pl.when(has_next)
    def _():
        guess_own.wait_send()
        guess_mate.wait_send()

    rate_mate.wait_send()

    @pl.when(has_low)
    def _():
        rate_low.wait_send()
        start_low.wait_send()

    @pl.when(has_high)
    def _():
        rate_high.wait_send()
        start_high.wait_send()

    sent(given, has_next)
    sent(passed, onward)
    defect_stay.wait()
    corrected_stay.wait()
    defect_go.wait()
    corrected_go.wait()


def on_device(nt, ns, initial, coarse_guess, react_rate):
    planes, across, width = initial.shape
    half = across // 2
    wide = -(-(2 * STEPS + max(nt - 2, 0)) // SUBLANES) * SUBLANES
    length = 2 * planes + 2 * STEPS
    field = pltpu.VMEM((length, half + 2 * wide, width), jnp.float32)
    shape = jax.ShapeDtypeStruct(initial.shape, jnp.float32)
    corrected, defect = pl.pallas_call(
        functools.partial(kernel, nt, ns, planes, half, wide),
        out_shape=(shape, shape),
        in_specs=[pl.BlockSpec(memory_space=pl.ANY)] * 3,
        out_specs=[pl.BlockSpec(memory_space=pl.ANY)] * 2,
        scratch_shapes=[field] * 11
        + [
            pltpu.VMEM((half + 2 * wide, width), jnp.float32),
            pltpu.SemaphoreType.DMA((COPIES + 2,)),
            pltpu.SemaphoreType.DMA((COPIES + 2,)),
            pltpu.SemaphoreType.DMA((4,)),
        ],
        compiler_params=pltpu.CompilerParams(collective_id=0, has_side_effects=True),
    )(initial, coarse_guess[0], react_rate)
    return corrected[None], defect[None]


def solution(mesh):
    in_specs = (P("space", None, None), P("tm", "space", None, None), P("space", None, None))
    out_specs = (P("tm", "space", None, None), P("tm", "space", None, None))
    return jax.shard_map(
        functools.partial(on_device, mesh.shape["tm"], mesh.shape["space"]),
        mesh=mesh, in_specs=in_specs, out_specs=out_specs, check_vma=False,
    )
```

time: 204 us -> 74.1 us (0.36)
  the two profiles are of different devices: /device:TPU:4 before, /device:TPU:13 now
where the time goes in v1:
time: 74.1 us; the launch traced here: 74 us
  Pallas kernels  70.5 us (95%)
  local copies, waits for them, and re-layouts  2.8 us (4%)
    pallas_call x1, Pallas kernels, on_device(): pl.pallas_call(functools.partial(kernel, nt, ns, planes, half, wide), out...  70.5 us
    unnamed x4, local copies, waits for them, and re-layouts  2.8 us

profile of v1, /device:TPU:13, one launch (start us, length us, event | category | flops | bytes accessed | tf_op | source)
XLA Modules:
  0.0 74.0 jit_solution(5915065257829346954)
XLA Ops:
  0.6 70.5 %shard_map.50 = (f32[3,192,256]{2,1,0:T(8,128)}, f32[3,192,256]{2,1,0:T(8,128)}) custom-call(f32[3,192,256]{2,1,0:T(8,128)} %initial.1, f32[3,192,256]{2,1,0:T(8,128)} %bitcast.3, f32[3,192,256]{2,1,0:T(8,128)} %rate_in.1), custom_call_target="tpu_custom_call" | custom-call | tf_op jit(solution)/shard_map/pallas_call | solution.py:365
  71.2 0.0 copy-start
  71.2 2.0 %copy.7 = f32[1,3,192,256]{3,2,1,0:T(8,128)} copy(f32[1,3,192,256]{3,2,1,0:T(8,128)} %bitcast.5) | data formatting | bytes 1179648
  73.2 0.0 copy-done
  73.2 0.8 %copy.8 = f32[1,3,192,256]{3,2,1,0:T(8,128)} copy(f32[1,3,192,256]{3,2,1,0:T(8,128)S(1)} %bitcast.4) | data formatting | bytes 1179648
Async XLA Ops:
  71.2 2.0 %copy-start = (f32[3,192,256]{2,1,0:T(8,128)S(1)}, f32[3,192,256]{2,1,0:T(8,128)}, u32[]{:S(2)}) copy-start(f32[3,192,256]{2,1,0:T(8,128)} %get-tuple-element.5) | copy-start | bytes 1769476

commit v2 on v1

--- a/solution.py
+++ b/solution.py
@@ -16,12 +16,23 @@
 
 MESH = pl.DeviceIdType.MESH
 
-START, RATE, AGAIN, CHAIN, DEFECT, CORRECTED = 0, 4, 8, 11, 14, 15
-COPIES = 16
+PIECES = 4
+
+
+def slots(planes):
+    kinds = dict(
+        start=4, start_edge=2, rate=1, rate_edge=2, again=PIECES, again_edge=2 * PIECES,
+        chain=2 * planes, chain_edge=2, defect=1, corrected=planes,
+    )
+    first, total = {}, 0
+    for kind, number in kinds.items():
+        first[kind] = total
+        total += number
+    return first, total
 
 
 def kernel(
-    nt, ns, planes, half, wide,
+    nt, ns, planes, half, wide, slot_of,
     initial, guess, rate_in, corrected_out, defect_out,
     start, rate, again, before, first, second, relaxed, coarse, offset, defect, after, reach,
     send, recv, local,
@@ -93,17 +104,17 @@
 
     rate_own = pltpu.make_async_copy(cut(rate_in, side), spot(rate, side, slab, planes), local.at[0])
     rate_mate = remote(
-        cut(rate_in, 1 - side), spot(rate, 1 - side, slab, planes), RATE, tm, mate
+        cut(rate_in, 1 - side), spot(rate, 1 - side, slab, planes), slot_of["rate"], tm, mate
     )
     initial_own = pltpu.make_async_copy(cut(initial, side), spot(start, side, slab, planes), local.at[1])
     initial_mate = remote(
-        cut(initial, 1 - side), spot(start, 1 - side, slab, planes), START, tm, mate
+        cut(initial, 1 - side), spot(start, 1 - side, slab, planes), slot_of["start"], tm, mate
     )
     guess_mate = remote(
-        cut(guess, 1 - side), spot(start, 1 - side, slab, planes), START + 3, tm + 1, mate
+        cut(guess, 1 - side), spot(start, 1 - side, slab, planes), slot_of["start"] + 3, tm + 1, mate
     )
     guess_own = remote(
-        cut(guess, side), spot(start, side, slab, planes), START + 2, tm + 1, space
+        cut(guess, side), spot(start, side, slab, planes), slot_of["start"] + 2, tm + 1, space
     )
 
     @pl.when(tm == 0)
@@ -156,8 +167,8 @@
         def _():
             high.start()
 
-    start_low, start_high = edges(start, STEPS, COPIES, tm)
-    rate_low, rate_high = edges(rate, STEPS - 1, RATE + 1, tm)
+    start_low, start_high = edges(start, STEPS, slot_of["start_edge"], tm)
+    rate_low, rate_high = edges(rate, STEPS - 1, slot_of["rate_edge"], tm)
 
     rate_own.wait()
     send_edge(rate_low, rate_high, side)
@@ -229,48 +240,62 @@
     fine(first, second, 2)
     fine(second, relaxed, 3)
 
-    def give(src, dst, width, slot):
-        whole = remote(
-            spot(src, side, STEPS, block), spot(dst, side, STEPS, block), slot, tm + 1, space
-        )
-        low = remote(
-            spot(src, side, STEPS, width), spot(dst, side, STEPS + block, width), slot + 1, tm + 1, space - 2
-        )
-        high = remote(
-            spot(src, side, STEPS + block - width, width),
-            spot(dst, side, STEPS - width, width),
-            slot + 2,
-            tm + 1,
-            space + 2,
-        )
-        return whole, low, high
-
-    def begin(copies, valid):
-        whole, low, high = copies
-        pl.when(jnp.logical_and(valid, has_low))(low.start)
-        pl.when(jnp.logical_and(valid, has_high))(high.start)
-        pl.when(valid)(whole.start)
-
-    def sent(copies, valid):
-        whole, low, high = copies
-        pl.when(jnp.logical_and(valid, has_low))(low.wait_send)
-        pl.when(jnp.logical_and(valid, has_high))(high.wait_send)
-        pl.when(valid)(whole.wait_send)
-
-    def received(copies, valid):
-        whole, low, high = copies
-        pl.when(jnp.logical_and(valid, has_high))(low.wait_recv)
-        pl.when(jnp.logical_and(valid, has_low))(high.wait_recv)
-        pl.when(valid)(whole.wait_recv)
-
-    given = give(relaxed, again, STEPS, AGAIN)
-    begin(given, has_next)
+    groups = (half + wide) // SUBLANES
+    bounds = [groups * piece // PIECES * SUBLANES for piece in range(PIECES + 1)]
+
+    def piece_of(ref, begin, size, piece):
+        at = pl.multiple_of(wide * (1 - side) + bounds[piece], SUBLANES)
+        return ref.at[pl.ds(begin, size), pl.ds(at, bounds[piece + 1] - bounds[piece]), :]
+
+    given, given_low, given_high = [], [], []
+    for piece in range(PIECES):
+        slot = slot_of["again_edge"] + 2 * piece
+        given.append(
+            remote(
+                piece_of(relaxed, STEPS, block, piece),
+                piece_of(again, STEPS, block, piece),
+                slot_of["again"] + piece,
+                tm + 1,
+                space,
+            )
+        )
+        given_low.append(
+            remote(
+                piece_of(again, STEPS, STEPS, piece),
+                piece_of(again, STEPS + block, STEPS, piece),
+                slot,
+                tm,
+                space - 2,
+            )
+        )
+        given_high.append(
+            remote(
+                piece_of(again, block, STEPS, piece),
+                piece_of(again, 0, STEPS, piece),
+                slot + 1,
+                tm,
+                space + 2,
+            )
+        )
+
+    @pl.when(has_next)
+    def _():
+        for piece in range(PIECES):
+            given[piece].start()
 
     @pl.when(tm == 0)
     def _():
         keep.wait()
 
-    received(given, has_previous)
+    @pl.when(has_previous)
+    def _():
+        for piece in range(PIECES):
+            given[piece].wait_recv()
+            pl.when(has_low)(given_low[piece].start)
+            pl.when(has_high)(given_high[piece].start)
+        for piece in range(PIECES):
+            pl.when(has_high)(given_low[piece].wait_recv)
+            pl.when(has_low)(given_high[piece].wait_recv)
 
     def first_plane(z, carry):
         middle, delta = change(again, z)
@@ -281,50 +306,109 @@
     lax.fori_loop(*span(1), first_plane, 0)
     fine(first, second, 2)
 
-    def last_plane(z, carry):
+    order = []
+    for depth in range(planes):
+        order += [STEPS + depth, STEPS + block - 1 - depth]
+
+    def row_span(z):
+        at = pl.multiple_of(wide * (1 - side), SUBLANES)
+        return (pl.ds(z, 1), pl.ds(at, half + wide), slice(None))
+
+    passed = {
+        z: remote(
+            after.at[row_span(z)], before.at[row_span(z)], slot_of["chain"] + z - STEPS, tm + 1, space
+        )
+        for z in order
+    }
+    low_edge, high_edge = STEPS, STEPS + block - 1
+    passed_low = remote(
+        before.at[row_span(low_edge)], before.at[row_span(high_edge + 1)],
+        slot_of["chain_edge"], tm, space - 2,
+    )
+    passed_high = remote(
+        before.at[row_span(high_edge)], before.at[row_span(low_edge - 1)],
+        slot_of["chain_edge"] + 1, tm, space + 2,
+    )
+
+    mine = pl.ds(pl.multiple_of(side * half, SUBLANES), half)
+    middle_rows = pl.ds(wide, half)
+    defect_stay = pltpu.make_async_copy(
+        defect.at[pl.ds(slab, planes), middle_rows, :], defect_out.at[:, mine, :], local.at[2]
+    )
+    defect_go = remote(
+        defect.at[pl.ds(other, planes), middle_rows, :], defect_out.at[:, mine, :],
+        slot_of["defect"], tm, mate,
+    )
+    stay, go = {}, {}
+    for z in order:
+        place = (z - STEPS) % planes
+        src = after.at[pl.ds(z, 1), middle_rows, :]
+        dst = corrected_out.at[pl.ds(place, 1), mine, :]
+        stay[z] = pltpu.make_async_copy(src, dst, local.at[3 + place])
+        go[z] = remote(src, dst, slot_of["corrected"] + place, tm, mate)
+
+    def at_home(z):
+        return side == (z - STEPS) // planes
+
+    def hand_in(z):
+        pl.when(at_home(z))(stay[z].start)
+        pl.when(jnp.logical_not(at_home(z)))(go[z].start)
+
+    def last_plane(z):
         middle, delta = change(second, z)
         end = middle + delta
         defect[z] = end - relaxed[z]
         shift = end - coarse[z]
         offset[z] = shift
         after[z] = coarse[z] + shift
-        return carry
-
-    lax.fori_loop(STEPS, STEPS + block, last_plane, 0)
-
-    def back(src, dst, slot, lane_slot):
-        mine = pl.ds(pl.multiple_of(side * half, SUBLANES), half)
-        middle_rows = pl.ds(wide, half)
-        stay = pltpu.make_async_copy(
-            src.at[pl.ds(slab, planes), middle_rows, :], dst.at[:, mine, :], local.at[lane_slot]
-        )
-        go = remote(
-            src.at[pl.ds(other, planes), middle_rows, :], dst.at[:, mine, :], slot, tm, mate
-        )
-        return stay, go
-
-    defect_stay, defect_go = back(defect, defect_out, DEFECT, 2)
-
-    passed = give(after, before, 1, CHAIN)
+
+    opens = jnp.logical_and(tm == 1, has_next)
+    for index, z in enumerate(order):
+        last_plane(z)
+        if index:
+            pl.when(opens)(passed[order[index - 1]].start)
+    pl.when(opens)(passed[order[-1]].start)
+    defect_go.start()
+    defect_stay.start()
+
     later = tm > 1
-    received(passed, later)
+
+    @pl.when(jnp.logical_not(later))
+    def _():
+        for z in order:
+            hand_in(z)
 
     @pl.when(later)
     def _():
-        def plane(z, carry):
+        queue = list(order)
+        waiting = set(order)
+
+        def leave(z):
+            pl.when(has_next)(passed[z].start)
+            hand_in(z)
+
+        for index, z in enumerate(order):
+            while waiting & {z - 1, z, z + 1}:
+                come = queue.pop(0)
+                waiting.remove(come)
+                passed[come].wait_recv()
+                if come == low_edge:
+                    pl.when(has_low)(passed_low.start)
+                if come == high_edge:
+                    pl.when(has_high)(passed_high.start)
+            if z == low_edge:
+                pl.when(has_low)(passed_high.wait_recv)
+            if z == high_edge:
+                pl.when(has_high)(passed_low.wait_recv)
             middle, delta = change(before, z)
             after[z] = middle + coarse_ratio * delta + offset[z]
-            return carry
-
-        lax.fori_loop(STEPS, STEPS + block, plane, 0)
+            if index:
+                leave(order[index - 1])
+        leave(order[-1])
+        pl.when(has_low)(passed_low.wait_send)
+        pl.when(has_high)(passed_high.wait_send)
 
     onward = jnp.logical_and(tm > 0, has_next)
-    begin(passed, onward)
-    defect_go.start()
-    defect_stay.start()
-    corrected_stay, corrected_go = back(after, corrected_out, CORRECTED, 3)
-    corrected_go.start()
-    corrected_stay.start()
 
     @pl.when(tm == 0)
     def _():
@@ -347,12 +431,28 @@
         rate_high.wait_send()
         start_high.wait_send()
 
-    sent(given, has_next)
-    sent(passed, onward)
+    @pl.when(has_next)
+    def _():
+        for piece in range(PIECES):
+            given[piece].wait_send()
+
+    @pl.when(has_previous)
+    def _():
+        for piece in range(PIECES):
+            pl.when(has_low)(given_low[piece].wait_send)
+            pl.when(has_high)(given_high[piece].wait_send)
+
+    @pl.when(onward)
+    def _():
+        for z in order:
+            passed[z].wait_send()
+
     defect_stay.wait()
-    corrected_stay.wait()
     defect_go.wait()
-    corrected_go.wait()
+    for z in order:
+        pl.when(at_home(z))(stay[z].wait)
+        pl.when(at_home(z))(go[z].wait_recv)
+        pl.when(jnp.logical_not(at_home(z)))(go[z].wait_send)
 
 
 def on_device(nt, ns, initial, coarse_guess, react_rate):
@@ -361,18 +461,19 @@
     wide = -(-(2 * STEPS + max(nt - 2, 0)) // SUBLANES) * SUBLANES
     length = 2 * planes + 2 * STEPS
     field = pltpu.VMEM((length, half + 2 * wide, width), jnp.float32)
+    slot_of, total = slots(planes)
     shape = jax.ShapeDtypeStruct(initial.shape, jnp.float32)
     corrected, defect = pl.pallas_call(
-        functools.partial(kernel, nt, ns, planes, half, wide),
+        functools.partial(kernel, nt, ns, planes, half, wide, slot_of),
         out_shape=(shape, shape),
         in_specs=[pl.BlockSpec(memory_space=pl.ANY)] * 3,
         out_specs=[pl.BlockSpec(memory_space=pl.ANY)] * 2,
         scratch_shapes=[field] * 11
         + [
             pltpu.VMEM((half + 2 * wide, width), jnp.float32),
-            pltpu.SemaphoreType.DMA((COPIES + 2,)),
-            pltpu.SemaphoreType.DMA((COPIES + 2,)),
-            pltpu.SemaphoreType.DMA((4,)),
+            pltpu.SemaphoreType.DMA((total,)),
+            pltpu.SemaphoreType.DMA((total,)),
+            pltpu.SemaphoreType.DMA((3 + planes,)),
         ],
         compiler_params=pltpu.CompilerParams(collective_id=0, has_side_effects=True),
     )(initial, coarse_guess[0], react_rate)

time: 74.1 us -> 64.2 us (0.87)
  Pallas kernels: 70.5 us -> 60.6 us
    pallas_call x1, Pallas kernels: 70.5 us -> 60.6 us  [on_device(): pl.pallas_call(functools.partial(kernel, nt, ns, planes, half, wide, slot...]
where the time goes in v2:
time: 64.2 us; the launch traced here: 64 us
  Pallas kernels  60.6 us (94%)
  local copies, waits for them, and re-layouts  2.8 us (4%)
  between operations  0.65 us (1%)
    pallas_call x1, Pallas kernels, on_device(): pl.pallas_call(functools.partial(kernel, nt, ns, planes, half, wide, slot...  60.6 us
    unnamed x4, local copies, waits for them, and re-layouts  2.8 us

profile of v2, /device:TPU:13, one launch (start us, length us, event | category | flops | bytes accessed | tf_op | source)
XLA Modules:
  0.0 64.0 jit_solution(15924249871811265382)
XLA Ops:
  0.6 60.6 %shard_map.50 = (f32[3,192,256]{2,1,0:T(8,128)}, f32[3,192,256]{2,1,0:T(8,128)}) custom-call(f32[3,192,256]{2,1,0:T(8,128)} %initial.1, f32[3,192,256]{2,1,0:T(8,128)} %bitcast.3, f32[3,192,256]{2,1,0:T(8,128)} %rate_in.1), custom_call_target="tpu_custom_call" | custom-call | tf_op jit(solution)/shard_map/pallas_call | solution.py:466
  61.2 0.0 copy-start
  61.2 2.0 %copy.7 = f32[1,3,192,256]{3,2,1,0:T(8,128)} copy(f32[1,3,192,256]{3,2,1,0:T(8,128)} %bitcast.5) | data formatting | bytes 1179648
  63.2 0.0 copy-done
  63.2 0.8 %copy.8 = f32[1,3,192,256]{3,2,1,0:T(8,128)} copy(f32[1,3,192,256]{3,2,1,0:T(8,128)S(1)} %bitcast.4) | data formatting | bytes 1179648
Async XLA Ops:
  61.2 2.0 %copy-start = (f32[3,192,256]{2,1,0:T(8,128)S(1)}, f32[3,192,256]{2,1,0:T(8,128)}, u32[]{:S(2)}) copy-start(f32[3,192,256]{2,1,0:T(8,128)} %get-tuple-element.5) | copy-start | bytes 1769476

commit v3 on v2

--- a/solution.py
+++ b/solution.py
@@ -21,7 +21,7 @@
 
 def slots(planes):
     kinds = dict(
-        start=4, start_edge=2, rate=1, rate_edge=2, again=PIECES, again_edge=2 * PIECES,
+        start=2 + PIECES, start_edge=1 + PIECES, rate=1, rate_edge=2, rate_core=3, again=PIECES, again_edge=2 * PIECES,
         chain=2 * planes, chain_edge=2, defect=1, corrected=planes,
     )
     first, total = {}, 0
@@ -80,6 +80,15 @@
             else:
                 pl.semaphore_signal(barrier, inc=1, device_id=target, device_id_type=MESH)
                 count = count + 1
+    for here, there in ((tm == 0, nt - 1), (tm == nt - 1, 0)):
+
+        @pl.when(here)
+        def _(there=there):
+            pl.semaphore_signal(
+                barrier, inc=1, device_id={"tm": there, "space": mate}, device_id_type=MESH
+            )
+
+        count = count + here.astype(jnp.int32)
     pl.semaphore_wait(barrier, count)
 
     def remote(src, dst, slot, to_tm, to_space):
@@ -102,33 +111,70 @@
     slab = STEPS + planes * side
     other = STEPS + planes * (1 - side)
 
+    core = lax.rem(tm, 2)
+    twin = tm + 1 - 2 * core
+    lanes = start.shape[2] // 2
+
+    def lane_half(ref, which):
+        return ref.at[:, :, pl.ds(pl.multiple_of(which * lanes, lanes), lanes)]
+
+    groups = (half + wide) // SUBLANES
+    bounds = [groups * piece // PIECES * SUBLANES for piece in range(PIECES + 1)]
+
+    def piece_of(ref, begin, size, piece, target=side):
+        at = pl.multiple_of(wide * (1 - target) + bounds[piece], SUBLANES)
+        return ref.at[pl.ds(begin, size), pl.ds(at, bounds[piece + 1] - bounds[piece]), :]
+
+    def cut_piece(ref, target, piece):
+        at = pl.multiple_of(target * (half - wide) + bounds[piece], SUBLANES)
+        return ref.at[:, pl.ds(at, bounds[piece + 1] - bounds[piece]), :]
+
     rate_own = pltpu.make_async_copy(cut(rate_in, side), spot(rate, side, slab, planes), local.at[0])
     rate_mate = remote(
-        cut(rate_in, 1 - side), spot(rate, 1 - side, slab, planes), slot_of["rate"], tm, mate
+        lane_half(cut(rate_in, 1 - side), core),
+        lane_half(spot(rate, 1 - side, slab, planes), core),
+        slot_of["rate"],
+        tm,
+        mate,
     )
     initial_own = pltpu.make_async_copy(cut(initial, side), spot(start, side, slab, planes), local.at[1])
-    initial_mate = remote(
-        cut(initial, 1 - side), spot(start, 1 - side, slab, planes), slot_of["start"], tm, mate
-    )
-    guess_mate = remote(
-        cut(guess, 1 - side), spot(start, 1 - side, slab, planes), slot_of["start"] + 3, tm + 1, mate
-    )
     guess_own = remote(
-        cut(guess, side), spot(start, side, slab, planes), slot_of["start"] + 2, tm + 1, space
-    )
+        cut(guess, side), spot(start, side, slab, planes), slot_of["start"], tm + 1, space
+    )
+
+    def to_mate(ref, to_tm):
+        return [
+            remote(
+                cut_piece(ref, 1 - side, piece),
+                piece_of(start, slab, planes, piece, 1 - side),
+                slot_of["start"] + 1 + piece,
+                to_tm,
+                mate,
+            )
+            for piece in range(PIECES)
+        ]
+
+    guess_mate = to_mate(guess, tm + 1)
+    initial_mate = to_mate(initial, 0)
+    is_last = tm == nt - 1
+
+    rate_mate.start()
+    rate_own.start()
+
+    @pl.when(has_next)
+    def _():
+        guess_own.start()
+        for copy in guess_mate:
+            copy.start()
+
+    @pl.when(is_last)
+    def _():
+        for copy in initial_mate:
+            copy.start()
 
     @pl.when(tm == 0)
     def _():
-        initial_mate.start()
         initial_own.start()
-
-    @pl.when(has_next)
-    def _():
-        guess_mate.start()
-        guess_own.start()
-
-    rate_own.start()
-    rate_mate.start()
 
     for ref in (first, second):
         @pl.when(jnp.logical_not(has_low))
@@ -145,33 +191,53 @@
     )
     reach[...] = jnp.where(outside, 0.0, fine_diffuse)
 
-    def edges(ref, width, slot, to_tm):
+    low_place, high_place = STEPS + block, 0
+
+    def edge_pieces(piece):
+        slot = slot_of["start_edge"] + 1 + piece
         low = remote(
-            spot(ref, side, STEPS, width), spot(ref, side, STEPS + block, width), slot, to_tm, space - 2
+            piece_of(start, STEPS, STEPS, piece), piece_of(start, low_place, STEPS, piece),
+            slot, tm, space - 2,
         )
         high = remote(
-            spot(ref, side, STEPS + block - width, width),
-            spot(ref, side, STEPS - width, width),
-            slot + 1,
-            to_tm,
-            space + 2,
+            piece_of(start, block, STEPS, piece), piece_of(start, high_place, STEPS, piece),
+            slot, tm, space + 2,
         )
         return low, high
 
-    def send_edge(low, high, which):
-        @pl.when(jnp.logical_and(which == 0, has_low))
-        def _():
-            low.start()
-
-        @pl.when(jnp.logical_and(which == 1, has_high))
-        def _():
-            high.start()
-
-    start_low, start_high = edges(start, STEPS, slot_of["start_edge"], tm)
-    rate_low, rate_high = edges(rate, STEPS - 1, slot_of["rate_edge"], tm)
+    start_edges = [edge_pieces(piece) for piece in range(PIECES)]
+    start_low = remote(
+        spot(start, side, STEPS, STEPS), spot(start, side, low_place, STEPS),
+        slot_of["start_edge"], tm, space - 2,
+    )
+    start_high = remote(
+        spot(start, side, block, STEPS), spot(start, side, high_place, STEPS),
+        slot_of["start_edge"], tm, space + 2,
+    )
+    reach_rate = STEPS - 1
+    rate_low_spot = lane_half(spot(rate, side, low_place, reach_rate), core)
+    rate_high_spot = lane_half(spot(rate, side, high_place + 1, reach_rate), core)
+    rate_low = remote(
+        lane_half(spot(rate, side, STEPS, reach_rate), core), rate_low_spot,
+        slot_of["rate_edge"], tm, space - 2,
+    )
+    rate_high = remote(
+        lane_half(spot(rate, side, STEPS + block - reach_rate, reach_rate), core), rate_high_spot,
+        slot_of["rate_edge"] + 1, tm, space + 2,
+    )
+    rate_other_spot = lane_half(spot(rate, side, other, planes), core)
+    twin_mate = remote(rate_other_spot, rate_other_spot, slot_of["rate_core"], twin, space)
+    twin_low = remote(rate_low_spot, rate_low_spot, slot_of["rate_core"] + 1, twin, space)
+    twin_high = remote(rate_high_spot, rate_high_spot, slot_of["rate_core"] + 2, twin, space)
+
+    own_low = jnp.logical_and(side == 0, has_low)
+    own_high = jnp.logical_and(side == 1, has_high)
+    other_low = jnp.logical_and(side == 1, has_low)
+    other_high = jnp.logical_and(side == 0, has_high)
 
     rate_own.wait()
-    send_edge(rate_low, rate_high, side)
+    pl.when(own_low)(rate_low.start)
+    pl.when(own_high)(rate_high.start)
 
     @pl.when(tm == 0)
     def _():
@@ -181,29 +247,50 @@
     def _():
         guess_own.wait_recv()
 
-    send_edge(start_low, start_high, side)
-
-    @pl.when(tm == 0)
-    def _():
-        initial_mate.wait_recv()
-
-    @pl.when(has_previous)
-    def _():
-        guess_mate.wait_recv()
-
-    send_edge(start_low, start_high, 1 - side)
+    pl.when(own_low)(start_low.start)
+    pl.when(own_high)(start_high.start)
+
     rate_mate.wait_recv()
-    send_edge(rate_low, rate_high, 1 - side)
+    pl.when(other_low)(rate_low.start)
+    pl.when(other_high)(rate_high.start)
+    twin_mate.start()
+
+    for piece in range(PIECES):
+        guess_mate[piece].wait_recv()
+        pl.when(other_low)(start_edges[piece][0].start)
+        pl.when(other_high)(start_edges[piece][1].start)
 
     @pl.when(has_high)
     def _():
         rate_low.wait_recv()
+        twin_low.start()
+
+    @pl.when(has_low)
+    def _():
+        rate_high.wait_recv()
+        twin_high.start()
+
+    twin_mate.wait_recv()
+    pl.when(has_high)(twin_low.wait_recv)
+    pl.when(has_low)(twin_high.wait_recv)
+
+    @pl.when(jnp.logical_and(side == 0, has_high))
+    def _():
         start_low.wait_recv()
 
-    @pl.when(has_low)
-    def _():
-        rate_high.wait_recv()
+    @pl.when(jnp.logical_and(side == 1, has_low))
+    def _():
         start_high.wait_recv()
+
+    @pl.when(jnp.logical_and(side == 1, has_high))
+    def _():
+        for low, high in start_edges:
+            low.wait_recv()
+
+    @pl.when(jnp.logical_and(side == 0, has_low))
+    def _():
+        for low, high in start_edges:
+            high.wait_recv()
 
     keep = pltpu.make_async_copy(start, again, local.at[1])
 
@@ -239,13 +326,6 @@
     fine(start, first, 1)
     fine(first, second, 2)
     fine(second, relaxed, 3)
-
-    groups = (half + wide) // SUBLANES
-    bounds = [groups * piece // PIECES * SUBLANES for piece in range(PIECES + 1)]
-
-    def piece_of(ref, begin, size, piece):
-        at = pl.multiple_of(wide * (1 - side) + bounds[piece], SUBLANES)
-        return ref.at[pl.ds(begin, size), pl.ds(at, bounds[piece + 1] - bounds[piece]), :]
 
     given, given_low, given_high = [], [], []
     for piece in range(PIECES):
@@ -410,26 +490,35 @@
 
     onward = jnp.logical_and(tm > 0, has_next)
 
-    @pl.when(tm == 0)
-    def _():
-        initial_mate.wait_send()
+    @pl.when(is_last)
+    def _():
+        for copy in initial_mate:
+            copy.wait_send()
 
     @pl.when(has_next)
     def _():
         guess_own.wait_send()
-        guess_mate.wait_send()
+        for copy in guess_mate:
+            copy.wait_send()
 
     rate_mate.wait_send()
-
-    @pl.when(has_low)
-    def _():
-        rate_low.wait_send()
-        start_low.wait_send()
-
-    @pl.when(has_high)
-    def _():
-        rate_high.wait_send()
-        start_high.wait_send()
+    twin_mate.wait_send()
+    pl.when(has_high)(twin_low.wait_send)
+    pl.when(has_low)(twin_high.wait_send)
+    pl.when(has_low)(rate_low.wait_send)
+    pl.when(has_high)(rate_high.wait_send)
+    pl.when(own_low)(start_low.wait_send)
+    pl.when(own_high)(start_high.wait_send)
+
+    @pl.when(other_low)
+    def _():
+        for low, high in start_edges:
+            low.wait_send()
+
+    @pl.when(other_high)
+    def _():
+        for low, high in start_edges:
+            high.wait_send()
 
     @pl.when(has_next)
     def _():

time: 64.2 us -> 57.1 us (0.89)
  Pallas kernels: 60.6 us -> 53.4 us
    pallas_call x1, Pallas kernels: 60.6 us -> 53.4 us  [on_device(): pl.pallas_call(functools.partial(kernel, nt, ns, planes, half, wide, slot...]
where the time goes in v3:
time: 57.1 us; the launch traced here: 56.9 us
  Pallas kernels  53.4 us (94%)
  local copies, waits for them, and re-layouts  2.8 us (5%)
  between operations  0.65 us (1%)
    pallas_call x1, Pallas kernels, on_device(): pl.pallas_call(functools.partial(kernel, nt, ns, planes, half, wide, slot...  53.4 us
    unnamed x4, local copies, waits for them, and re-layouts  2.8 us

profile of v3, /device:TPU:13, one launch (start us, length us, event | category | flops | bytes accessed | tf_op | source)
XLA Modules:
  0.0 56.9 jit_solution(11424561251409476099)
XLA Ops:
  0.6 53.4 %shard_map.50 = (f32[3,192,256]{2,1,0:T(8,128)}, f32[3,192,256]{2,1,0:T(8,128)}) custom-call(f32[3,192,256]{2,1,0:T(8,128)} %initial.1, f32[3,192,256]{2,1,0:T(8,128)} %bitcast.3, f32[3,192,256]{2,1,0:T(8,128)} %rate_in.1), custom_call_target="tpu_custom_call" | custom-call | tf_op jit(solution)/shard_map/pallas_call | solution.py:555
  54.0 0.0 copy-start
  54.1 2.0 %copy.7 = f32[1,3,192,256]{3,2,1,0:T(8,128)} copy(f32[1,3,192,256]{3,2,1,0:T(8,128)} %bitcast.5) | data formatting | bytes 1179648
  56.0 0.0 copy-done
  56.0 0.8 %copy.8 = f32[1,3,192,256]{3,2,1,0:T(8,128)} copy(f32[1,3,192,256]{3,2,1,0:T(8,128)S(1)} %bitcast.4) | data formatting | bytes 1179648
Async XLA Ops:
  54.0 2.0 %copy-start = (f32[3,192,256]{2,1,0:T(8,128)S(1)}, f32[3,192,256]{2,1,0:T(8,128)}, u32[]{:S(2)}) copy-start(f32[3,192,256]{2,1,0:T(8,128)} %get-tuple-element.5) | copy-start | bytes 1769476

commit v4 on v3

--- a/solution.py
+++ b/solution.py
@@ -442,6 +442,13 @@
         offset[z] = shift
         after[z] = coarse[z] + shift
 
+    def take_edges():
+        passed[low_edge].wait_recv()
+        pl.when(has_low)(passed_low.start)
+        passed[high_edge].wait_recv()
+        pl.when(has_high)(passed_high.start)
+
+    pl.when(tm == 2)(take_edges)
     opens = jnp.logical_and(tm == 1, has_next)
     for index, z in enumerate(order):
         last_plane(z)
@@ -460,8 +467,9 @@
 
     @pl.when(later)
     def _():
-        queue = list(order)
-        waiting = set(order)
+        pl.when(tm > 2)(take_edges)
+        queue = order[2:]
+        waiting = set(queue)
 
         def leave(z):
             pl.when(has_next)(passed[z].start)
@@ -472,10 +480,6 @@
                 come = queue.pop(0)
                 waiting.remove(come)
                 passed[come].wait_recv()
-                if come == low_edge:
-                    pl.when(has_low)(passed_low.start)
-                if come == high_edge:
-                    pl.when(has_high)(passed_high.start)
             if z == low_edge:
                 pl.when(has_low)(passed_high.wait_recv)
             if z == high_edge:

time: 57.1 us -> 56.3 us (0.986)
  Pallas kernels: 53.4 us -> 52.6 us
    pallas_call x1, Pallas kernels: 53.4 us -> 52.6 us  [on_device(): pl.pallas_call(functools.partial(kernel, nt, ns, planes, half, wide, slot...]
where the time goes in v4:
time: 56.3 us; the launch traced here: 56 us
  Pallas kernels  52.6 us (93%)
  local copies, waits for them, and re-layouts  2.8 us (5%)
  between operations  0.65 us (1%)
    pallas_call x1, Pallas kernels, on_device(): pl.pallas_call(functools.partial(kernel, nt, ns, planes, half, wide, slot...  52.6 us
    unnamed x4, local copies, waits for them, and re-layouts  2.8 us

profile of v4, /device:TPU:13, one launch (start us, length us, event | category | flops | bytes accessed | tf_op | source)
XLA Modules:
  0.0 56.0 jit_solution(17644408517439981220)
XLA Ops:
  0.6 52.6 %shard_map.50 = (f32[3,192,256]{2,1,0:T(8,128)}, f32[3,192,256]{2,1,0:T(8,128)}) custom-call(f32[3,192,256]{2,1,0:T(8,128)} %initial.1, f32[3,192,256]{2,1,0:T(8,128)} %bitcast.3, f32[3,192,256]{2,1,0:T(8,128)} %rate_in.1), custom_call_target="tpu_custom_call" | custom-call | tf_op jit(solution)/shard_map/pallas_call | solution.py:559
  53.2 0.0 copy-start
  53.2 2.0 %copy.7 = f32[1,3,192,256]{3,2,1,0:T(8,128)} copy(f32[1,3,192,256]{3,2,1,0:T(8,128)} %bitcast.5) | data formatting | bytes 1179648
  55.2 0.0 copy-done
  55.2 0.8 %copy.8 = f32[1,3,192,256]{3,2,1,0:T(8,128)} copy(f32[1,3,192,256]{3,2,1,0:T(8,128)S(1)} %bitcast.4) | data formatting | bytes 1179648
Async XLA Ops:
  53.2 2.0 %copy-start = (f32[3,192,256]{2,1,0:T(8,128)S(1)}, f32[3,192,256]{2,1,0:T(8,128)}, u32[]{:S(2)}) copy-start(f32[3,192,256]{2,1,0:T(8,128)} %get-tuple-element.5) | copy-start | bytes 1769476
